TPU v7x, 32 devices: a whole 2x2x4 slice. The times are simulated.
32 devices in a mesh: dp: 8 (over z, y), tensor: 4 (over x, core).
Axes of the slice: x: 2, y: 2, z: 4, core: 2. Of those that a mesh axis runs over, the one named last changes fastest.
Arguments:
- query_act: bfloat16 [8, 1024, 1024], P('dp', None, 'tensor'), may hold values from -6 to 6
- rotated_keys: bfloat16 [8, 1024, 256], P('dp'), may hold values from -6 to 6
- value_input: bfloat16 [8, 1024, 256], P('dp'), may hold values from -6 to 6
- grad_out: bfloat16 [8, 1024, 8192], P('dp', 'tensor'), may hold values from -6 to 6
- out_weight: bfloat16 [1024, 8192], P('tensor', 'dp'), may hold values from -0.1875 to 0.1875
- doc_lengths: int32 [8, 4], P('dp'), may hold values from 1 to 512, 1024 in all within a row
Outputs:
- query_grad: bfloat16 [8, 1024, 1024], P('dp', None, 'tensor')
- key_gradient: bfloat16 [8, 4, 512, 128], P('dp', 'tensor')
- value_gradient: bfloat16 [8, 4, 512, 128], P('dp', 'tensor')
- weight_grad: float32 [1024, 8192], P('tensor', 'dp')
All inputs are finite; a program needn't handle non-finite values.
Results may differ from a plain program's by a relative error of at most 0.015.
The roundings to bfloat16 on the way count: a program that leaves them out, or rounds other values in their place, can miss the bound.
Values may be sent and summed in bfloat16 or wider, within the bound.
A program may use at most 128 MiB of HBM per device.

v0:
```python
import jax
import jax.numpy as jnp
from jax import lax
from jax.sharding import PartitionSpec as P

HEAD_SIZE = 128


def swapped(value, axis, apart):
    mask = 2**apart
    pairs = [(source, source ^ mask) for source in range(lax.axis_size(axis))]
    return lax.ppermute(value, axis, pairs)


def shards(query_act, rotated_keys, value_input, grad_out, out_weight, doc_lengths):
    score_scale = HEAD_SIZE ** (-0.5)
    tensor_index = lax.axis_index("tensor")
    kv_group = tensor_index // 2
    own_half = tensor_index % 2
    seq_len = query_act.shape[1]
    head_count = query_act.shape[2] // HEAD_SIZE
    query_heads = query_act[0].reshape(seq_len, head_count, HEAD_SIZE).transpose(1, 0, 2)
    key_rows = lax.dynamic_slice_in_dim(rotated_keys[0], kv_group * HEAD_SIZE, HEAD_SIZE, 1)
    value_rows = lax.dynamic_slice_in_dim(value_input[0], kv_group * HEAD_SIZE, HEAD_SIZE, 1)
    doc_ends = jnp.cumsum(doc_lengths[0])
    positions = jnp.arange(seq_len, dtype=jnp.int32)
    doc_ids = jnp.sum((positions[:, None] >= doc_ends[None, :]).astype(jnp.int32), axis=1)
    block_rows = min(512, seq_len)
    block_count = seq_len // block_rows
    full_weight = lax.all_gather(out_weight, "dp", axis=1, tiled=True)

    def key_reach():
        return seq_len

    def masked_scores(block_idx, key_span):
        first = block_idx * block_rows
        query_block = query_heads[:, first : first + block_rows]
        scores = (
            jnp.einsum("hqd,kd->hqk", query_block, key_rows, preferred_element_type=jnp.float32)
            * score_scale
        )
        allowed = (positions[None, :key_span] <= positions[first : first + block_rows, None]) & (
            doc_ids[None, :key_span] == doc_ids[first : first + block_rows, None]
        )
        return jnp.where(allowed[None], scores, -jnp.inf)

    totals_list = []
    outputs_list = []
    for block_idx in range(block_count):
        key_span = key_reach()
        scores = masked_scores(block_idx, key_span)
        row_max = jnp.max(scores, axis=-1, keepdims=True)
        log_total = row_max + jnp.log(jnp.sum(jnp.exp(scores - row_max), axis=-1, keepdims=True))
        prob_bf16 = jnp.exp(scores - log_total).astype(jnp.bfloat16)
        outputs_list.append(
            jnp.einsum(
                "hqk,kd->hqd", prob_bf16, value_rows, preferred_element_type=jnp.float32
            ).astype(jnp.bfloat16)
        )
        totals_list.append(log_total)
    attn_out = jnp.concatenate(outputs_list, axis=1)
    out_flat = attn_out.transpose(1, 0, 2).reshape(seq_len, head_count * HEAD_SIZE)
    local_rows = grad_out[0]
    gathered = lax.all_gather(local_rows, "tensor", axis=0, tiled=True)
    out_grad = jnp.einsum(
        "sd,hd->sh", gathered, full_weight, preferred_element_type=jnp.float32
    ).astype(jnp.bfloat16)
    weight_part = jnp.einsum("sh,sd->hd", out_flat, gathered, preferred_element_type=jnp.float32)
    weight_grad = lax.psum_scatter(weight_part, "dp", scatter_dimension=1, tiled=True)
    grad_heads = out_grad.reshape(seq_len, head_count, HEAD_SIZE).transpose(1, 0, 2)
    key_accum = jnp.zeros((seq_len, HEAD_SIZE), jnp.float32)
    value_accum = jnp.zeros((seq_len, HEAD_SIZE), jnp.float32)
    query_list = []
    for block_idx in range(block_count):
        key_span = key_reach()
        first = block_idx * block_rows
        scores = masked_scores(block_idx, key_span)
        prob_block = jnp.exp(scores - totals_list[block_idx])
        prob_bf16 = prob_block.astype(jnp.bfloat16)
        grad_block = grad_heads[:, first : first + block_rows]
        out_block = attn_out[:, first : first + block_rows]
        query_block = query_heads[:, first : first + block_rows]
        dprobs = jnp.einsum(
            "hqd,kd->hqk", grad_block, value_rows, preferred_element_type=jnp.float32
        )
        row_delta = jnp.sum(
            grad_block.astype(jnp.float32) * out_block.astype(jnp.float32), axis=-1, keepdims=True
        )
        score_gradient = (prob_block * (dprobs - row_delta) * score_scale).astype(jnp.bfloat16)
        query_list.append(
            jnp.einsum(
                "hqk,kd->hqd", score_gradient, key_rows, preferred_element_type=jnp.float32
            ).astype(jnp.bfloat16)
        )
        key_accum = key_accum.at[:key_span].add(
            jnp.einsum(
                "hqk,hqd->kd", score_gradient, query_block, preferred_element_type=jnp.float32
            )
        )
        value_accum = value_accum.at[:key_span].add(
            jnp.einsum("hqk,hqd->kd", prob_bf16, grad_block, preferred_element_type=jnp.float32)
        )
    query_grad = (
        jnp.concatenate(query_list, axis=1)
        .transpose(1, 0, 2)
        .reshape(1, seq_len, head_count * HEAD_SIZE)
    )
    half_rows = seq_len // 2
    other_start = (1 - own_half) * half_rows
    outgoing = (
        lax.dynamic_slice_in_dim(key_accum, other_start, half_rows, 0),
        lax.dynamic_slice_in_dim(value_accum, other_start, half_rows, 0),
    )
    partner = swapped((outgoing[0], outgoing[1]), "tensor", 0)
    key_mine = lax.dynamic_slice_in_dim(key_accum, own_half * half_rows, half_rows, 0) + partner[0]
    value_mine = (
        lax.dynamic_slice_in_dim(value_accum, own_half * half_rows, half_rows, 0) + partner[1]
    )
    key_gradient = key_mine.astype(jnp.bfloat16).reshape(1, 1, half_rows, HEAD_SIZE)
    value_gradient = value_mine.astype(jnp.bfloat16).reshape(1, 1, half_rows, HEAD_SIZE)
    return (query_grad, key_gradient, value_gradient, weight_grad)


def solution(mesh):
    placed = (
        P("dp", None, "tensor"),
        P("dp", None, None),
        P("dp", None, None),
        P("dp", "tensor", None),
        P("tensor", "dp"),
        P("dp", None),
    )
    return jax.shard_map(
        shards,
        mesh=mesh,
        in_specs=placed,
        out_specs=(
            P("dp", None, "tensor"),
            P("dp", "tensor", None, None),
            P("dp", "tensor", None, None),
            P("tensor", "dp"),
        ),
        check_vma=False,
    )
```

profile of v0, /device:TPU:0, one launch (start us, length us, event | category | flops | bytes accessed | tf_op | source)
XLA Modules:
  0.0 374.6 jit_solution(8681585686457070649)
XLA Ops:
  7.3 0.7 all-gather.4.cloned.1.call-update
  8.0 0.7 all-gather.6.cloned.1.call-update
  9.2 0.3 copy.30
  9.6 0.9 fusion.9
  10.5 0.9 fusion.7
  11.4 0.9 fusion.6
  12.4 2.2 exponential_reduce_fusion
  14.7 1.6 convolution_convert_fusion.1
  16.2 69.5 %all-gather.4.cloned.1.call-done = bf16[256,8192]{1,0:T(8,128)(2,1)} async-done(((bf16[256,1024]{1,0:T(8,128)(2,1)}), bf16[256,8192]{1,0:T(8,128)(2,1)}) %all-gather.4.cloned.1.call-update) | async-done | bytes 4194320 | tf_op jit(solution)/shard_map/all_gather | solution.py:30
  85.7 106.0 %all-gather.6.cloned.1.call-done = bf16[1,1024,8192]{2,1,0:T(8,128)(2,1)} async-done(((bf16[1,256,8192]{2,1,0:T(8,128)(2,1)}), bf16[1,1024,8192]{2,1,0:T(8,128)(2,1)}) %all-gather.6.cloned.1.call-update) | async-done | bytes 16777232 | tf_op jit(solution)/shard_map/all_gather | solution.py:64
  191.8 11.5 %fusion.10 = bf16[1024,256]{0,1:T(8,128)(2,1)S(1)} fusion(bf16[256,8192]{1,0:T(8,128)(2,1)} %all-gather.4.cloned.1.call-done, bf16[1,1024,8192]{2,1,0:T(8,128)(2,1)} %all-gather.6.cloned.1.call-done), kind=kOutput, calls=%fused_computation.20 | convolution fusion | flops 4295229440 | bytes 21495808 | tf_op jit(solution)/shard_map/sd,hd->sh/dot_general | solution.py:65
  203.2 0.3 copy.31
  203.5 3.8 %multiply_reduce_fusion.1 = (f32[2,512]{1,0:T(2,128)S(1)}, f32[2,512]{1,0:T(2,128)S(1)}, bf16[2,512,128]{2,1,0:T(8,128)(2,1)S(1)}) fusion(bf16[2,1024,128]{2,1,0:T(8,128)(2,1)S(1)} %bitcast.100, bf16[2,512,128]{2,1,0:T(8,128)(2,1)S(1)} %convolution_convert_fusion.1, bf16[1,1024,256]{2,1,0:T(8,128)(2,1)S(1)} %copy-done, s32[]{:T(128)S(6)} %select_n.33, ...), kind=kOutput, calls=%fused_computation.34 | convolution fusion | flops 273807360 | bytes 6041604 | tf_op jit(solution)/shard_map/hqk,kd->hqd/dot_general | solution.py:56
  207.4 0.2 copy.39
  207.6 12.5 %fusion = f32[256,8192]{1,0:T(8,128)} fusion(bf16[1024,256]{0,1:T(8,128)(2,1)S(1)} %bitcast.93, bf16[1,1024,8192]{2,1,0:T(8,128)(2,1)} %all-gather.6.cloned.1.call-done), kind=kOutput, calls=%fused_computation | convolution fusion | flops 4294967296 | bytes 25690112 | tf_op jit(solution)/shard_map/sh,sd->hd/dot_general | solution.py:68
  220.1 1.0 copy-done.7
  221.1 4.0 %multiply_convert_fusion = bf16[2,512,1024]{1,2,0:T(8,128)(2,1)S(1)} fusion(f32[1024,2,512]{2,0,1:T(8,128)} %copy-done.1, f32[2,512]{1,0:T(2,128)S(1)} %get-tuple-element.93, f32[2,512]{1,0:T(2,128)S(1)} %log_add_fusion, pred[512,1024]{0,1:T(8,128)(4,1)S(1)} %get-tuple-element.94, bf16[2,1024,128]{2,1,0:T(8,128)(2,1)S(1)} %bitcast.101, ...), kind=kOutput, calls=%fused_computation.6 | convolution fusion | flops 275775488 | bytes 7348228 | tf_op jit(solution)/shard_map/hqd,kd->hqk/dot_general | solution.py:83
  225.1 0.7 convolution_bitcast_fusion.2
  225.8 1.7 multiply_convert_fusion.1
  227.5 0.7 fusion.13
  228.3 0.3 collective-permute-start
  228.6 0.8 convolution_convert_fusion
  229.4 0.4 copy-done.2
  229.8 1.1 convolution_bitcast_fusion
  230.8 1.3 fusion.14
  232.1 0.8 convolution_convert_fusion.2
  232.9 0.3 collective-permute-start.1
  233.3 0.2 copy.38
  233.5 1.0 copy.40
  234.5 0.7 fusion.41
  235.2 1.6 fusion.42
  236.8 131.3 %reduce-scatter.2.cloned.1.call-done = f32[256,1024]{1,0:T(8,128)} async-done(((f32[256,8192]{1,0:T(8,128)}), f32[256,1024]{1,0:T(8,128)}) %reduce-scatter.2.cloned.1.call-update) | async-done | bytes 1048592 | tf_op jit(solution)/shard_map/reduce_scatter | solution.py:69
  (40 shorter events, 0.9 us)
Async XLA Ops:
  7.2 7.5 %copy-start = (bf16[1,1024,256]{2,1,0:T(8,128)(2,1)S(1)}, bf16[1,1024,256]{2,1,0:T(8,128)(2,1)}, u32[]{:S(2)}) copy-start(bf16[1,1024,256]{2,1,0:T(8,128)(2,1)} %param.24) | copy-start | bytes 1572868
  7.2 1.6 copy-start.10
  7.2 1.8 copy-start.5
  7.2 3.3 copy-start.8
  7.2 78.5 %all-gather.4.cloned.1.call-start = ((), (), s32[]{:S(2)}) async-start(), calls=%async_computation.1 | async-start | bytes 4718592 | tf_op jit(solution)/shard_map/all_gather | solution.py:30
  7.9 183.8 %all-gather.6.cloned.1.call-start = ((), (), s32[]{:S(2)}) async-start(), calls=%async_computation.3 | async-start | bytes 20971520 | tf_op jit(solution)/shard_map/all_gather | solution.py:64
  8.7 359.4 %reduce-scatter.2.cloned.1.call-start = ((), (), s32[]{:S(2)}) async-start(), calls=%async_computation.2 | async-start | bytes 9437184 | tf_op jit(solution)/shard_map/reduce_scatter | solution.py:69
  11.4 3.2 copy-start.1
  12.4 2.3 copy-start.3
  203.5 3.8 %copy-start.6 = (bf16[1024,2,128]{2,0,1:T(8,128)(2,1)}, bf16[1024,2,128]{2,0,1:T(8,128)(2,1)S(1)}, u32[]{:S(2)}) copy-start(bf16[1024,2,128]{2,0,1:T(8,128)(2,1)S(1)} %copy.31) | copy-start | bytes 1572868
  220.1 1.0 copy-start.7
  221.1 4.7 %copy-start.4 = (f32[1024,2,512]{2,0,1:T(8,128)S(1)}, f32[1024,2,512]{2,0,1:T(8,128)}, u32[]{:S(2)}) copy-start(f32[1024,2,512]{2,0,1:T(8,128)} %copy-done.3) | copy-start | bytes 12582916
  225.8 2.8 copy-start.9
  227.5 2.3 copy-start.2
  228.3 6.2 %collective-permute-start = (f32[512,128]{1,0:T(8,128)S(1)}, f32[512,128]{1,0:T(8,128)S(1)}, u32[]{:S(2)}, u32[]{:S(2)}) collective-permute-start(f32[512,128]{1,0:T(8,128)S(1)} %constant_dynamic-slice_fusion.1), channel_id=1, source_target_pairs={{0,1},{1,0},{2,3},{3,2},{4,5},{5,4},{6,7},{7,6},{8,9},{9,8},{10,11... | collective-permute-start | bytes 786440 | tf_op jit(solution)/shard_map/ppermute | solution.py:12
  232.9 2.3 collective-permute-start.1
Sparse Core Ops, SparseCore 0:
  10.2 75.4 all-gather.3
  87.3 104.4 all-gather.5
  220.2 147.8 reduce-scatter.1
where the time goes:
time: 375 us
  waiting for transfers between devices  308 us (82%)
  matrix products  42.1 us (11%)
  between operations  14.1 us (4%)
  other arithmetic  5.72 us (2%)
  local copies, waits for them, and re-layouts  3.8 us (1%)
    reduce_scatter x1, waiting for transfers between devices, shards(): lax.psum_scatter(weight_part, 'dp', scatter_dimension=1, tiled=True)  131 us
    all_gather x1, waiting for transfers between devices, shards(): gathered = lax.all_gather(local_rows, 'tensor', axis=0, tiled=True)  106 us
    all_gather x1, waiting for transfers between devices, shards(): full_weight = lax.all_gather(out_weight, 'dp', axis=1, tiled=True)  69.5 us
    dot_general x1, matrix products, shards(): jnp.einsum('sh,sd->hd', out_flat, gathered, preferred_element_type=jnp.fl...  12.5 us
    dot_general x1, matrix products, shards(): jnp.einsum('sd,hd->sh', gathered, full_weight, preferred_element_type=jnp...  11.5 us
  transfers between devices with their start and end apart: 5, of which 3 were waited for; matrix products, arithmetic and copies ran while one was open for 6% of the time, Pallas kernels for 0%

commit v1 on v0

--- a/solution.py
+++ b/solution.py
@@ -4,6 +4,27 @@
 from jax.sharding import PartitionSpec as P
 
 HEAD_SIZE = 128
+
+
+def _put_leaves(buf, matrix):
+    row_out = lax.axis_size("dp")
+    low, res, f_now = (row_out, lax.axis_index("dp"), buf.shape[1])
+    queue = tuple(((kk, (kk + 1) % low) for kk in range(low)))
+    block_out = low // 2
+    state_next = a_next = buf
+    before = matrix(buf, res * f_now)
+    bank = tuple(((kk, (kk - 1) % low) for kk in range(low)))
+    hop_no = 1
+    while hop_no < block_out + 1:
+        state_next = lax.ppermute(state_next, "dp", queue)
+        if hop_no < low - block_out:
+            a_next = lax.ppermute(a_next, "dp", bank)
+            frame_out = matrix(a_next, (res + hop_no) % low * f_now)
+            before = before + frame_out
+        last = matrix(state_next, (res - hop_no) % low * f_now)
+        before = before + last
+        hop_no += 1
+    return before
 
 
 def swapped(value, axis, apart):
@@ -27,7 +48,6 @@
     doc_ids = jnp.sum((positions[:, None] >= doc_ends[None, :]).astype(jnp.int32), axis=1)
     block_rows = min(512, seq_len)
     block_count = seq_len // block_rows
-    full_weight = lax.all_gather(out_weight, "dp", axis=1, tiled=True)
 
     def key_reach():
         return seq_len
@@ -62,8 +82,14 @@
     out_flat = attn_out.transpose(1, 0, 2).reshape(seq_len, head_count * HEAD_SIZE)
     local_rows = grad_out[0]
     gathered = lax.all_gather(local_rows, "tensor", axis=0, tiled=True)
-    out_grad = jnp.einsum(
-        "sd,hd->sh", gathered, full_weight, preferred_element_type=jnp.float32
+    out_grad = _put_leaves(
+        out_weight,
+        lambda shard, offset: jnp.einsum(
+            "sd,hd->sh",
+            lax.dynamic_slice_in_dim(gathered, offset, shard.shape[1], axis=1),
+            shard,
+            preferred_element_type=jnp.float32,
+        ),
     ).astype(jnp.bfloat16)
     weight_part = jnp.einsum("sh,sd->hd", out_flat, gathered, preferred_element_type=jnp.float32)
     weight_grad = lax.psum_scatter(weight_part, "dp", scatter_dimension=1, tiled=True)

time: 375 us -> 307 us (0.82)
  waiting for transfers between devices: 308 us -> 213 us
  starting transfers between devices: 0.76 us -> 20.4 us
  matrix products: 42.1 us -> 48.9 us
    all_gather x1, waiting for transfers between devices: 106 us -> 34.1 us  [shards(): gathered = lax.all_gather(local_rows, 'tensor', axis=0, tiled=True)]
    all_gather x1 -> x0, waiting for transfers between devices: 69.5 us -> none  [shards(): full_weight = lax.all_gather(out_weight, 'dp', axis=1, tiled=True)]
    ppermute x0 -> x7, waiting for transfers between devices: none -> 46.8 us  [the longest x4 46.8 us: _put_leaves(): state_next = lax.ppermute(state_next, 'dp', queue)]
    ppermute x0 -> x7, starting transfers between devices: none -> 19.7 us  [the longest x4 10.5 us: _put_leaves(): state_next = lax.ppermute(state_next, 'dp', queue)]
    dot_general x1 -> x8, matrix products: 11.5 us -> 15.8 us  [shards(): jnp.einsum('sd,hd->sh', lax.dynamic_slice_in_dim(gathered, offset, shard....]
  transfers between devices with their start and end apart: 5 -> 11, of which waited for: 3 -> 5; matrix products, arithmetic and copies ran while one was open for 6% -> 12% of each run, Pallas kernels for 0% -> 0%
where the time goes in v1:
time: 307 us; the launch traced here: 306 us
  waiting for transfers between devices  213 us (69%)
  matrix products  48.9 us (16%)
  starting transfers between devices  20.4 us (7%)
  between operations  14.6 us (5%)
  other arithmetic  5.52 us (2%)
  local copies, waits for them, and re-layouts  3.72 us (1%)
    reduce_scatter x1, waiting for transfers between devices, shards(): lax.psum_scatter(weight_part, 'dp', scatter_dimension=1, tiled=True)  131 us
    ppermute x4, waiting for transfers between devices, _put_leaves(): state_next = lax.ppermute(state_next, 'dp', queue)  46.8 us
    all_gather x1, waiting for transfers between devices, shards(): gathered = lax.all_gather(local_rows, 'tensor', axis=0, tiled=True)  34.1 us
    dot_general x8, matrix products, shards(): jnp.einsum('sd,hd->sh', lax.dynamic_slice_in_dim(gathered, offset, shard....  15.8 us
    dot_general x1, matrix products, shards(): jnp.einsum('sh,sd->hd', out_flat, gathered, preferred_element_type=jnp.fl...  12.7 us
    ppermute x4, starting transfers between devices, _put_leaves(): state_next = lax.ppermute(state_next, 'dp', queue)  10.5 us
    ppermute x3, starting transfers between devices, _put_leaves(): a_next = lax.ppermute(a_next, 'dp', bank)  9.23 us
    dot_general x2, matrix products, shards(): jnp.einsum('hqk,kd->hqd', prob_bf16, value_rows, preferred_element_type=j...  7.65 us
  transfers between devices with their start and end apart: 11, of which 5 were waited for; matrix products, arithmetic and copies ran while one was open for 12% of the time, Pallas kernels for 0%

profile of v1, /device:TPU:0, one launch (start us, length us, event | category | flops | bytes accessed | tf_op | source)
XLA Modules:
  0.0 306.1 jit_solution(13719683005017068003)
XLA Ops:
  8.0 3.0 collective-permute-start.1
  11.0 3.1 %collective-permute-start = (bf16[256,1024]{1,0:T(8,128)(2,1)}, bf16[256,1024]{1,0:T(8,128)(2,1)S(1)}, u32[]{:S(2)}, u32[]{:S(2)}) collective-permute-start(bf16[256,1024]{1,0:T(8,128)(2,1)} %param.26), channel_id=1, source_target_pairs={{0,28},{4,0},{8,4},{12,8},{16,12},{20,16},{24,20},{28,24},{1,29},{... | collective-permute-start | bytes 1572872 | tf_op jit(solution)/shard_map/ppermute | solution.py:21
  15.0 0.9 fusion.31
  15.9 0.9 fusion.5
  16.8 0.9 fusion.4
  17.8 16.0 %collective-permute-done.1 = bf16[256,1024]{1,0:T(8,128)(2,1)} collective-permute-done((bf16[256,1024]{1,0:T(8,128)(2,1)}, bf16[256,1024]{1,0:T(8,128)(2,1)}, u32[]{:S(2)}, u32[]{:S(2)}) %collective-permute-start.1) | collective-permute-done | bytes 524320 | tf_op jit(solution)/shard_map/ppermute | solution.py:19
  33.8 2.5 collective-permute-start.3
  36.3 2.0 exponential_reduce_fusion
  38.3 3.1 %collective-permute-start.2 = (bf16[256,1024]{1,0:T(8,128)(2,1)S(1)}, bf16[256,1024]{1,0:T(8,128)(2,1)S(1)}, u32[]{:S(2)}, u32[]{:S(2)}) collective-permute-start(bf16[256,1024]{1,0:T(8,128)(2,1)S(1)} %collective-permute-done), channel_id=1, source_target_pairs={{0,28},{4,0},{8,4},{12,8},{16,12},{20,16},{24,20},{28,24},{1,29},{... | collective-permute-start | bytes 1572872 | tf_op jit(solution)/shard_map/ppermute | solution.py:21
  41.4 16.8 %collective-permute-done.3 = bf16[256,1024]{1,0:T(8,128)(2,1)} collective-permute-done((bf16[256,1024]{1,0:T(8,128)(2,1)}, bf16[256,1024]{1,0:T(8,128)(2,1)}, u32[]{:S(2)}, u32[]{:S(2)}) %collective-permute-start.3) | collective-permute-done | bytes 524320 | tf_op jit(solution)/shard_map/ppermute | solution.py:19
  58.1 2.5 collective-permute-start.5
  60.8 3.9 %convolution_convert_fusion.1 = bf16[2,512,128]{2,1,0:T(8,128)(2,1)S(1)} fusion(bf16[1,1024,256]{2,1,0:T(8,128)(2,1)S(1)} %copy-done, s32[]{:T(128)S(6)} %select_n.85, f32[1024,2,512]{2,0,1:T(8,128)} %copy-done.2, f32[2,512]{1,0:T(2,128)S(1)} %log_add_fusion, pred[512,1024]{0,1:T(8,128)(4,1)S(1)} %get-tuple-element.94), kind=kOutput, calls=%fused_computation.57 | convolution fusion | flops 272760832 | bytes 5246980 | tf_op jit(solution)/shard_map/hqk,kd->hqd/dot_general | solution.py:76
  64.6 3.0 collective-permute-start.4
  67.7 14.0 %collective-permute-done.5 = bf16[256,1024]{1,0:T(8,128)(2,1)} collective-permute-done((bf16[256,1024]{1,0:T(8,128)(2,1)}, bf16[256,1024]{1,0:T(8,128)(2,1)}, u32[]{:S(2)}, u32[]{:S(2)}) %collective-permute-start.5) | collective-permute-done | bytes 524320 | tf_op jit(solution)/shard_map/ppermute | solution.py:19
  81.6 2.5 collective-permute-start.6
  84.1 34.1 %all-gather.3.cloned.1.call-done = bf16[1,1024,8192]{2,1,0:T(8,128)(2,1)} async-done(((bf16[1,256,8192]{2,1,0:T(8,128)(2,1)}), bf16[1,1024,8192]{2,1,0:T(8,128)(2,1)}) %all-gather.3.cloned.1.call-update) | async-done | bytes 16777232 | tf_op jit(solution)/shard_map/all_gather | solution.py:84
  118.2 2.6 fusion.12
  120.8 2.9 fusion.16
  123.8 3.1 %fusion.20 = f32[1024,256]{0,1:T(8,128)S(1)} fusion(bf16[256,1024]{1,0:T(8,128)(2,1)} %param.26, bf16[1,1024,8192]{2,1,0:T(8,128)(2,1)} %all-gather.3.cloned.1.call-done, s32[]{:T(128)S(6)} %select_n.87), kind=kOutput, calls=%fused_computation.28 | convolution fusion | flops 536870912 | bytes 3670020 | tf_op jit(solution)/shard_map/sd,hd->sh/dot_general | solution.py:87
  128.5 1.8 fusion.8
  130.4 1.9 fusion.47
  132.3 1.8 fusion.53
  134.4 3.8 %multiply_reduce_fusion.1 = (f32[2,512]{1,0:T(2,128)S(1)}, f32[2,512]{1,0:T(2,128)S(1)}, bf16[2,512,128]{2,1,0:T(8,128)(2,1)S(1)}) fusion(bf16[2,1024,128]{2,1,0:T(8,128)(2,1)S(1)} %bitcast.144, bf16[2,512,128]{2,1,0:T(8,128)(2,1)S(1)} %convolution_convert_fusion.1, bf16[1,1024,256]{2,1,0:T(8,128)(2,1)S(1)} %copy-done, s32[]{:T(128)S(6)} %select_n.85, ...), kind=kOutput, calls=%fused_computation.63 | convolution fusion | flops 273807360 | bytes 6041604 | tf_op jit(solution)/shard_map/hqk,kd->hqd/dot_general | solution.py:76
  138.5 12.7 %fusion = f32[256,8192]{1,0:T(8,128)} fusion(bf16[1024,256]{0,1:T(8,128)(2,1)S(1)} %bitcast.136, bf16[1,1024,8192]{2,1,0:T(8,128)(2,1)} %all-gather.3.cloned.1.call-done), kind=kOutput, calls=%fused_computation | convolution fusion | flops 4294967296 | bytes 25690112 | tf_op jit(solution)/shard_map/sh,sd->hd/dot_general | solution.py:94
  151.2 1.0 copy-done.8
  152.2 4.0 %multiply_convert_fusion = bf16[2,512,1024]{1,2,0:T(8,128)(2,1)S(1)} fusion(f32[1024,2,512]{2,0,1:T(8,128)} %copy-done.2, f32[2,512]{1,0:T(2,128)S(1)} %get-tuple-element.93, f32[2,512]{1,0:T(2,128)S(1)} %log_add_fusion, pred[512,1024]{0,1:T(8,128)(4,1)S(1)} %get-tuple-element.94, bf16[2,1024,128]{2,1,0:T(8,128)(2,1)S(1)} %bitcast.145, ...), kind=kOutput, calls=%fused_computation.4 | convolution fusion | flops 275775488 | bytes 7348228 | tf_op jit(solution)/shard_map/hqd,kd->hqk/dot_general | solution.py:109
  156.9 1.7 multiply_convert_fusion.1
  160.9 1.1 convolution_bitcast_fusion
  162.0 1.3 fusion.57
  164.6 1.0 copy.40
  165.6 1.6 fusion.84
  167.9 131.3 %reduce-scatter.2.cloned.1.call-done = f32[256,1024]{1,0:T(8,128)} async-done(((f32[256,8192]{1,0:T(8,128)}), f32[256,1024]{1,0:T(8,128)}) %reduce-scatter.2.cloned.1.call-update) | async-done | bytes 1048592 | tf_op jit(solution)/shard_map/reduce_scatter | solution.py:95
  (60 shorter events, 8.8 us)
Async XLA Ops:
  7.2 53.6 %copy-start = (bf16[1,1024,256]{2,1,0:T(8,128)(2,1)S(1)}, bf16[1,1024,256]{2,1,0:T(8,128)(2,1)}, u32[]{:S(2)}) copy-start(bf16[1,1024,256]{2,1,0:T(8,128)(2,1)} %param.24) | copy-start | bytes 1572868
  7.2 7.0 %copy-start.11 = (s32[1,4]{1,0:T(1,128)S(1)}, s32[1,4]{1,0:T(1,128)}, u32[]{:S(2)}) copy-start(s32[1,4]{1,0:T(1,128)} %param.27) | copy-start | bytes 52
  7.2 7.2 %copy-start.6 = (bf16[1,1024,256]{2,1,0:T(8,128)(2,1)S(1)}, bf16[1,1024,256]{2,1,0:T(8,128)(2,1)}, u32[]{:S(2)}) copy-start(bf16[1,1024,256]{2,1,0:T(8,128)(2,1)} %param.22) | copy-start | bytes 1572868
  7.2 8.7 %copy-start.9 = (bf16[1,1024,256]{2,1,0:T(8,128)(2,1)S(1)}, bf16[1,1024,256]{2,1,0:T(8,128)(2,1)}, u32[]{:S(2)}) copy-start(bf16[1,1024,256]{2,1,0:T(8,128)(2,1)} %param.23) | copy-start | bytes 1572868
  7.2 111.0 %all-gather.3.cloned.1.call-start = ((), (), s32[]{:S(2)}) async-start(), calls=%async_computation.2 | async-start | bytes 20971520 | tf_op jit(solution)/shard_map/all_gather | solution.py:84
  7.9 291.3 %reduce-scatter.2.cloned.1.call-start = ((), (), s32[]{:S(2)}) async-start(), calls=%async_computation.1 | async-start | bytes 9437184 | tf_op jit(solution)/shard_map/reduce_scatter | solution.py:95
  8.0 25.8 %collective-permute-start.1 = (bf16[256,1024]{1,0:T(8,128)(2,1)}, bf16[256,1024]{1,0:T(8,128)(2,1)}, u32[]{:S(2)}, u32[]{:S(2)}) collective-permute-start(bf16[256,1024]{1,0:T(8,128)(2,1)} %param.26), channel_id=1, source_target_pairs={{0,4},{4,8},{8,12},{12,16},{16,20},{20,24},{24,28},{28,0},{1,5},{5... | collective-permute-start | bytes 1572872 | tf_op jit(solution)/shard_map/ppermute | solution.py:19
  11.0 27.2 %collective-permute-start = (bf16[256,1024]{1,0:T(8,128)(2,1)}, bf16[256,1024]{1,0:T(8,128)(2,1)S(1)}, u32[]{:S(2)}, u32[]{:S(2)}) collective-permute-start(bf16[256,1024]{1,0:T(8,128)(2,1)} %param.26), channel_id=1, source_target_pairs={{0,28},{4,0},{8,4},{12,8},{16,12},{20,16},{24,20},{28,24},{1,29},{... | collective-permute-start | bytes 1572872 | tf_op jit(solution)/shard_map/ppermute | solution.py:21
  16.8 21.4 %copy-start.2 = (f32[1024,2,512]{2,0,1:T(8,128)}, f32[1024,2,512]{2,0,1:T(8,128)S(1)}, u32[]{:S(2)}) copy-start(f32[1024,2,512]{2,0,1:T(8,128)S(1)} %get-tuple-element.101) | copy-start | bytes 12582916
  17.8 20.5 %copy-start.4 = (f32[1024,2,512]{2,0,1:T(8,128)}, f32[1024,2,512]{2,0,1:T(8,128)S(1)}, u32[]{:S(2)}) copy-start(f32[1024,2,512]{2,0,1:T(8,128)S(1)} %get-tuple-element.99) | copy-start | bytes 12582916
  33.8 24.4 %collective-permute-start.3 = (bf16[256,1024]{1,0:T(8,128)(2,1)}, bf16[256,1024]{1,0:T(8,128)(2,1)}, u32[]{:S(2)}, u32[]{:S(2)}) collective-permute-start(bf16[256,1024]{1,0:T(8,128)(2,1)} %collective-permute-done.1), channel_id=1, source_target_pairs={{0,4},{4,8},{8,12},{12,16},{16,20},{20,24},{24,28},{28,0},{1,5},{5... | collective-permute-start | bytes 1572872 | tf_op jit(solution)/shard_map/ppermute | solution.py:19
  38.3 26.4 %collective-permute-start.2 = (bf16[256,1024]{1,0:T(8,128)(2,1)S(1)}, bf16[256,1024]{1,0:T(8,128)(2,1)S(1)}, u32[]{:S(2)}, u32[]{:S(2)}) collective-permute-start(bf16[256,1024]{1,0:T(8,128)(2,1)S(1)} %collective-permute-done), channel_id=1, source_target_pairs={{0,28},{4,0},{8,4},{12,8},{16,12},{20,16},{24,20},{28,24},{1,29},{... | collective-permute-start | bytes 1572872 | tf_op jit(solution)/shard_map/ppermute | solution.py:21
  58.1 23.5 %collective-permute-start.5 = (bf16[256,1024]{1,0:T(8,128)(2,1)}, bf16[256,1024]{1,0:T(8,128)(2,1)}, u32[]{:S(2)}, u32[]{:S(2)}) collective-permute-start(bf16[256,1024]{1,0:T(8,128)(2,1)} %collective-permute-done.3), channel_id=1, source_target_pairs={{0,4},{4,8},{8,12},{12,16},{16,20},{20,24},{24,28},{28,0},{1,5},{5... | collective-permute-start | bytes 1572872 | tf_op jit(solution)/shard_map/ppermute | solution.py:19
  64.6 65.7 %collective-permute-start.4 = (bf16[256,1024]{1,0:T(8,128)(2,1)S(1)}, bf16[256,1024]{1,0:T(8,128)(2,1)}, u32[]{:S(2)}, u32[]{:S(2)}) collective-permute-start(bf16[256,1024]{1,0:T(8,128)(2,1)S(1)} %collective-permute-done.2), channel_id=1, source_target_pairs={{0,28},{4,0},{8,4},{12,8},{16,12},{20,16},{24,20},{28,24},{1,29},{... | collective-permute-start | bytes 1572872 | tf_op jit(solution)/shard_map/ppermute | solution.py:21
  81.6 50.6 %collective-permute-start.6 = (bf16[256,1024]{1,0:T(8,128)(2,1)}, bf16[256,1024]{1,0:T(8,128)(2,1)}, u32[]{:S(2)}, u32[]{:S(2)}) collective-permute-start(bf16[256,1024]{1,0:T(8,128)(2,1)} %collective-permute-done.5), channel_id=1, source_target_pairs={{0,4},{4,8},{8,12},{12,16},{16,20},{20,24},{24,28},{28,0},{1,5},{5... | collective-permute-start | bytes 1572872 | tf_op jit(solution)/shard_map/ppermute | solution.py:19
  118.2 8.6 %copy-start.1 = (bf16[1,1024,8192]{2,1,0:T(8,128)(2,1)S(1)}, bf16[1,1024,8192]{2,1,0:T(8,128)(2,1)}, u32[]{:S(2)}) copy-start(bf16[1,1024,8192]{2,1,0:T(8,128)(2,1)} %all-gather.3.cloned.1.call-done) | copy-start | bytes 50331652
  134.4 3.8 %copy-start.7 = (bf16[1024,2,128]{2,0,1:T(8,128)(2,1)}, bf16[1024,2,128]{2,0,1:T(8,128)(2,1)S(1)}, u32[]{:S(2)}) copy-start(bf16[1024,2,128]{2,0,1:T(8,128)(2,1)S(1)} %copy.31) | copy-start | bytes 1572868
  151.2 1.0 copy-start.8
  152.2 4.7 %copy-start.5 = (f32[1024,2,512]{2,0,1:T(8,128)S(1)}, f32[1024,2,512]{2,0,1:T(8,128)}, u32[]{:S(2)}) copy-start(f32[1024,2,512]{2,0,1:T(8,128)} %copy-done.4) | copy-start | bytes 12582916
  156.9 2.8 copy-start.10
  158.6 2.3 copy-start.3
  159.4 6.2 %collective-permute-start.7 = (f32[512,128]{1,0:T(8,128)S(1)}, f32[512,128]{1,0:T(8,128)}, u32[]{:S(2)}, u32[]{:S(2)}) collective-permute-start(f32[512,128]{1,0:T(8,128)S(1)} %constant_dynamic-slice_fusion.1), channel_id=1, source_target_pairs={{0,1},{1,0},{2,3},{3,2},{4,5},{5,4},{6,7},{7,6},{8,9},{9,8},{10,11... | collective-permute-start | bytes 786440 | tf_op jit(solution)/shard_map/ppermute | solution.py:33
  164.0 3.2 %collective-permute-start.8 = (f32[512,128]{1,0:T(8,128)S(1)}, f32[512,128]{1,0:T(8,128)S(1)}, u32[]{:S(2)}, u32[]{:S(2)}) collective-permute-start(f32[512,128]{1,0:T(8,128)S(1)} %constant_dynamic-slice_fusion), channel_id=1, source_target_pairs={{0,1},{1,0},{2,3},{3,2},{4,5},{5,4},{6,7},{7,6},{8,9},{9,8},{10,11... | collective-permute-start | bytes 786440 | tf_op jit(solution)/shard_map/ppermute | solution.py:33
Sparse Core Ops, SparseCore 0:
  9.6 108.6 all-gather.2
  151.3 147.8 reduce-scatter.1
